TPU v7x, 128 devices: a whole 4x4x4 slice. The times are simulated.
128 devices in a mesh: expert: 32 (over z, x, core), replica: 4 (over y).
Axes of the slice: x: 4, y: 4, z: 4, core: 2. Of those that a mesh axis runs over, the one named last changes fastest.
Arguments:
- atom_rows: bfloat16 [16384, 512], P(('expert', 'replica')), may hold values from -6 to 6
- grad_out: bfloat16 [16384, 512], P(('expert', 'replica')), may hold values from -6 to 6
- expert_ids: int32 [16384, 1], P(('expert', 'replica')), may hold values from 0 to 31; in each aligned block of 128 rows (0 to 127, 128 to 255, ...) at most 8 rows name the same one
- weight_in: bfloat16 [32, 512, 4096], P('expert', None, 'replica'), may hold values from -0.25 to 0.25
- weight_out: bfloat16 [32, 4096, 512], P('expert', 'replica'), may hold values from -0.09375 to 0.09375
Outputs:
- grad_atoms: bfloat16 [16384, 512], P(('expert', 'replica'))
- grad_weight_in: float32 [32, 512, 4096], P('expert', None, 'replica')
- grad_weight_out: float32 [32, 4096, 512], P('expert', 'replica')
Inputs may be any that keep to these rules, and one draw needn't show every extreme that they name: `expert_ids`: in each aligned block of 128 rows (the rows of one device) no expert is named by more than 8 rows, and in some block one expert is named by exactly 8 rows; every expert is named somewhere.
All inputs are finite; a program needn't handle non-finite values.
Results may differ from a plain program's by a relative error of at most 0.0049.
Values may be sent and summed in bfloat16 or wider, within the bound.
No kernel may reach another device: no remote copies, remote signals or barrier semaphores. Data moves between devices by JAX's collectives and lax.ppermute only.
A program may use at most 64 MiB of HBM per device.

v0:
```python
import jax
import jax.numpy as jnp
from jax import lax
from jax.sharding import PartitionSpec as P


def pack_table(expert_ids, experts, capacity):
    labels = expert_ids[:, 0]
    onehot = (labels[:, None] == jnp.arange(experts, dtype=jnp.int32)[None, :]).astype(jnp.int32)
    position = jnp.sum((jnp.cumsum(onehot, axis=0) - onehot) * onehot, axis=1)
    slot_index = labels * capacity + position
    return jnp.arange(experts * capacity, dtype=jnp.int32)[:, None] == slot_index[None, :]


def expert_backward(rows_in, rows_grad, weight_first, weight_second):
    preact = jnp.dot(rows_in, weight_first, preferred_element_type=jnp.float32)
    gate_sig = jax.nn.sigmoid(preact)
    activation = (preact * gate_sig).astype(jnp.bfloat16)
    grad_act = lax.dot_general(
        rows_grad, weight_second, (((1,), (1,)), ((), ())), preferred_element_type=jnp.float32
    )
    grad_pre = (grad_act * gate_sig * (1.0 + preact * (1.0 - gate_sig))).astype(jnp.bfloat16)
    grad_first = lax.dot_general(
        rows_in, grad_pre, (((0,), (0,)), ((), ())), preferred_element_type=jnp.float32
    )
    grad_second = lax.dot_general(
        activation, rows_grad, (((0,), (0,)), ((), ())), preferred_element_type=jnp.float32
    )
    partial_value = lax.dot_general(
        grad_pre, weight_first, (((1,), (1,)), ((), ())), preferred_element_type=jnp.float32
    )
    return (grad_first, grad_second, partial_value)


def body(atom_rows, grad_out, expert_ids, weight_in, weight_out):
    experts = lax.axis_size("expert")
    replicas = lax.axis_size("replica")
    local_rows = atom_rows.shape[0]
    width = atom_rows.shape[1]
    capacity = 2 * local_rows // experts
    slot_table = pack_table(expert_ids, experts, capacity)
    joined = jnp.concatenate([atom_rows, grad_out], axis=1)
    packed = jnp.dot(
        slot_table.astype(jnp.bfloat16), joined, preferred_element_type=jnp.float32
    ).astype(jnp.bfloat16)
    copies = jnp.broadcast_to(
        packed.reshape(experts, 1, capacity, 2 * width), (experts, replicas, capacity, 2 * width)
    )
    copies = copies.reshape(experts * replicas * capacity, 2 * width)
    arrived = lax.all_to_all(copies, ("expert", "replica"), split_axis=0, concat_axis=0, tiled=True)
    grad_first, grad_second, partial_value = expert_backward(
        arrived[:, :width], arrived[:, width:], weight_in[0], weight_out[0]
    )
    returned = lax.all_to_all(
        partial_value, ("expert", "replica"), split_axis=0, concat_axis=0, tiled=True
    )
    summed = jnp.sum(returned.reshape(experts, replicas, capacity, width), axis=1).reshape(
        experts * capacity, width
    )
    grad_rows = lax.dot_general(
        slot_table.astype(jnp.float32),
        summed,
        (((0,), (0,)), ((), ())),
        precision=lax.Precision.HIGHEST,
        preferred_element_type=jnp.float32,
    )
    return (grad_rows.astype(jnp.bfloat16), grad_first[None], grad_second[None])


def solution(mesh):
    return jax.shard_map(
        body,
        mesh=mesh,
        in_specs=(
            P(("expert", "replica"), None),
            P(("expert", "replica"), None),
            P(("expert", "replica"), None),
            P("expert", None, "replica"),
            P("expert", "replica", None),
        ),
        out_specs=(
            P(("expert", "replica"), None),
            P("expert", None, "replica"),
            P("expert", "replica", None),
        ),
        check_vma=False,
    )
```

profile of v0, /device:TPU:1, one launch (start us, length us, event | category | flops | bytes accessed | tf_op | source)
XLA Modules:
  0.0 90.2 jit_solution(9257330931481306880)
XLA Ops:
  0.6 0.0 copy-start
  0.6 0.8 fusion.19
  1.5 0.2 reduce_window_sum.11
  1.6 0.8 select_reduce_fusion
  2.5 0.7 multiply_add_fusion
  3.1 1.2 %fusion.4 = bf16[32,8,1024]{2,1,0:T(8,128)(2,1)S(1)} fusion(bf16[128,512]{1,0:T(8,128)(2,1)} %param.6, bf16[128,512]{1,0:T(8,128)(2,1)} %param.5, s32[128]{0:T(128)S(1)} %multiply_add_fusion), kind=kOutput, calls=%fused_computation.10 | convolution fusion | flops 67928064 | bytes 786944 | tf_op jit(solution)/shard_map/dot_general | solution.py:43
  4.4 0.3 broadcast_in_dim.17
  4.7 41.8 %all_to_all.18 = bf16[128,8,1024]{2,1,0:T(8,128)(2,1)S(1)} all-to-all(bf16[128,8,1024]{2,1,0:T(8,128)(2,1)S(1)} %bitcast.28), channel_id=1, replica_groups=mesh['expert'=32,'replica'=4] {'expert','replica'}, dimensions={0} | all-to-all | bytes 4194304 | tf_op jit(solution)/shard_map/all_to_all | solution.py:50
  46.5 0.0 copy-start.1
  46.5 0.0 copy-done
  46.5 0.0 copy-start.4
  46.5 1.3 %fusion.6 = f32[1024,1024]{1,0:T(8,128)S(1)} fusion(bf16[1,512,1024]{2,1,0:T(8,128)(2,1)S(1)} %copy-done, bf16[1024,1024]{1,0:T(8,128)(2,1)S(1)} %bitcast.29), kind=kOutput, calls=%fused_computation.13 | convolution fusion | flops 1073741824 | bytes 6291456 | tf_op jit(solution)/shard_map/dot_general | solution.py:16
  47.8 0.1 copy-done.1
  47.8 0.6 copy-done.4
  48.5 0.0 copy-start.5
  48.5 2.1 %multiply_convert_fusion.1 = bf16[1024,1024]{1,0:T(8,128)(2,1)S(1)} fusion(f32[1024,1024]{1,0:T(8,128)S(1)} %fusion.6, bf16[1,1024,512]{2,1,0:T(8,128)(2,1)S(1)} %copy-done.4, bf16[1024,1024]{1,0:T(8,128)(2,1)S(1)} %bitcast.30), kind=kOutput, calls=%fused_computation.1 | convolution fusion | flops 1083179008 | bytes 8388608 | tf_op jit(solution)/shard_map/dot_general | solution.py:19
  50.6 0.0 copy-done.5
  50.6 0.0 copy-start.3
  50.6 1.3 %copy-done.3 = bf16[1024,1024]{1,0:T(8,128)(2,1)} copy-done((bf16[1024,1024]{1,0:T(8,128)(2,1)}, bf16[1024,1024]{1,0:T(8,128)(2,1)S(1)}, u32[]{:S(2)}) %copy-start.3) | copy-done | bytes 2097176
  52.0 2.6 %fusion = f32[128,8,512]{2,1,0:T(8,128)} fusion(bf16[1024,1024]{1,0:T(8,128)(2,1)S(1)} %multiply_convert_fusion.1, bf16[1,512,1024]{2,1,0:T(8,128)(2,1)S(1)} %copy-done), kind=kOutput, calls=%fused_computation.4 | convolution fusion | flops 1073741824 | bytes 5242880 | tf_op jit(solution)/shard_map/dot_general | solution.py:29
  54.6 3.8 %all-to-all-start.1 = ((f32[128,8,512]{2,1,0:T(8,128)}), f32[128,8,512]{2,1,0:T(8,128)S(1)}, u32[]{:S(2)}, u32[]{:S(2)}) async-start(f32[128,8,512]{2,1,0:T(8,128)} %fusion), calls=%async_computation.1 | async-start | bytes 4194304 | tf_op jit(solution)/shard_map/all_to_all | solution.py:54
  58.4 0.0 copy-start.2
  58.4 4.6 %convolution_bitcast_fusion = f32[1,512,1024]{2,1,0:T(8,128)} fusion(bf16[1024,1024]{1,0:T(8,128)(2,1)} %copy-done.3, bf16[1024,1024]{1,0:T(8,128)(2,1)} %bitcast.31), kind=kOutput, calls=%fused_computation.7 | convolution fusion | flops 1073741824 | bytes 5242880 | tf_op jit(solution)/shard_map/dot_general | solution.py:23
  63.1 0.0 copy-done.2
  63.1 4.9 %fusion.3 = f32[1,1024,512]{2,1,0:T(8,128)} fusion(f32[1024,1024]{1,0:T(8,128)} %copy-done.5, bf16[1024,1024]{1,0:T(8,128)(2,1)S(1)} %bitcast.32), kind=kOutput, calls=%fused_computation.8 | convolution fusion | flops 1078984704 | bytes 7340032 | tf_op jit(solution)/shard_map/dot_general | solution.py:26
  67.9 21.0 %all-to-all-done.1 = f32[128,8,512]{2,1,0:T(8,128)S(1)} async-done(((f32[128,8,512]{2,1,0:T(8,128)}), f32[128,8,512]{2,1,0:T(8,128)S(1)}, u32[]{:S(2)}, u32[]{:S(2)}) %all-to-all-start.1) | async-done | bytes 2097184 | tf_op jit(solution)/shard_map/all_to_all | solution.py:54
  88.9 0.2 bitcast_reduce_fusion
  89.2 1.0 %convolution_convert_fusion.1 = bf16[128,512]{1,0:T(8,128)(2,1)} fusion(f32[32,8,512]{2,1,0:T(8,128)S(1)} %bitcast_reduce_fusion, s32[128]{0:T(128)S(1)} %multiply_add_fusion), kind=kOutput, calls=%fused_computation.11 | convolution fusion | flops 201424896 | bytes 655872 | tf_op jit(solution)/shard_map/dot_general | solution.py:60
Async XLA Ops:
  0.6 45.9 %copy-start = (bf16[1,512,1024]{2,1,0:T(8,128)(2,1)S(1)}, bf16[1,512,1024]{2,1,0:T(8,128)(2,1)}, u32[]{:S(2)}) copy-start(bf16[1,512,1024]{2,1,0:T(8,128)(2,1)} %param.8) | copy-start | bytes 3145732
  46.5 1.3 %copy-start.1 = (bf16[128,8,1024]{2,1,0:T(8,128)(2,1)}, bf16[128,8,1024]{2,1,0:T(8,128)(2,1)S(1)}, u32[]{:S(2)}) copy-start(bf16[128,8,1024]{2,1,0:T(8,128)(2,1)S(1)} %all_to_all.18) | copy-start | bytes 6291460
  46.5 2.0 %copy-start.4 = (bf16[1,1024,512]{2,1,0:T(8,128)(2,1)S(1)}, bf16[1,1024,512]{2,1,0:T(8,128)(2,1)}, u32[]{:S(2)}) copy-start(bf16[1,1024,512]{2,1,0:T(8,128)(2,1)} %param.9) | copy-start | bytes 3145732
  48.5 2.1 %copy-start.5 = (f32[1024,1024]{1,0:T(8,128)}, f32[1024,1024]{1,0:T(8,128)S(1)}, u32[]{:S(2)}) copy-start(f32[1024,1024]{1,0:T(8,128)S(1)} %fusion.6) | copy-start | bytes 12582916
  50.6 1.3 %copy-start.3 = (bf16[1024,1024]{1,0:T(8,128)(2,1)}, bf16[1024,1024]{1,0:T(8,128)(2,1)S(1)}, u32[]{:S(2)}) copy-start(bf16[1024,1024]{1,0:T(8,128)(2,1)S(1)} %multiply_convert_fusion.1) | copy-start | bytes 6291460
  54.6 34.4 %all-to-all-start.1 = ((f32[128,8,512]{2,1,0:T(8,128)}), f32[128,8,512]{2,1,0:T(8,128)S(1)}, u32[]{:S(2)}, u32[]{:S(2)}) async-start(f32[128,8,512]{2,1,0:T(8,128)} %fusion), calls=%async_computation.1 | async-start | bytes 4194304 | tf_op jit(solution)/shard_map/all_to_all | solution.py:54
  58.4 4.7 %copy-start.2 = (bf16[128,8,1024]{2,1,0:T(8,128)(2,1)S(1)}, bf16[128,8,1024]{2,1,0:T(8,128)(2,1)}, u32[]{:S(2)}) copy-start(bf16[128,8,1024]{2,1,0:T(8,128)(2,1)} %copy-done.1) | copy-start | bytes 6291460
where the time goes:
time: 90.5 us; the launch traced here: 90.2 us
  blocking collectives  41.8 us (46%)
  waiting for transfers between devices  21 us (23%)
  matrix products  17.8 us (20%)
  starting transfers between devices  3.82 us (4%)
  other arithmetic  2.71 us (3%)
  local copies, waits for them, and re-layouts  2.31 us (3%)
    all_to_all x1, blocking collectives, body(): lax.all_to_all(copies, ('expert', 'replica'), split_axis=0, concat_axis=0...  41.8 us
    all_to_all x1, waiting for transfers between devices, body(): lax.all_to_all(partial_value, ('expert', 'replica'), split_axis=0, concat...  21 us
    dot_general x1, matrix products, expert_backward(): lax.dot_general(activation, rows_grad, (((0,), (0,)), ((), ())), preferre...  4.85 us
    dot_general x1, matrix products, expert_backward(): lax.dot_general(rows_in, grad_pre, (((0,), (0,)), ((), ())), preferred_el...  4.64 us
    all_to_all x1, starting transfers between devices, body(): lax.all_to_all(partial_value, ('expert', 'replica'), split_axis=0, concat...  3.82 us
    dot_general x1, matrix products, expert_backward(): lax.dot_general(grad_pre, weight_first, (((1,), (1,)), ((), ())), preferr...  2.61 us
    dot_general x1, matrix products, expert_backward(): lax.dot_general(rows_grad, weight_second, (((1,), (1,)), ((), ())), prefe...  2.13 us
    unnamed x12, local copies, waits for them, and re-layouts  2.05 us
  transfers between devices with their start and end apart: 1, of which 1 were waited for; matrix products, arithmetic and copies ran while one was open for 11% of the time, Pallas kernels for 0%

commit v1 on v0

v1 whole, which is shorter than its diff:
```python
import functools

import jax
import jax.numpy as jnp
from jax import lax
from jax.experimental import pallas as pl
from jax.experimental.pallas import tpu as pltpu
from jax.sharding import PartitionSpec as P

VMEM = pltpu.VMEM


def slots_of(labels, experts, capacity):
    rows = labels.shape[1]
    named = lax.broadcasted_iota(jnp.int32, (experts, rows), 0) == labels
    earlier = lax.broadcasted_iota(jnp.int32, (rows, rows), 0) < lax.broadcasted_iota(jnp.int32, (rows, rows), 1)
    before = jnp.dot(
        named.astype(jnp.float32).astype(jnp.bfloat16),
        earlier.astype(jnp.float32).astype(jnp.bfloat16),
        preferred_element_type=jnp.float32,
    )
    place = jnp.sum(jnp.where(named, before, 0.0), axis=0, keepdims=True)
    return labels * capacity + place.astype(jnp.int32)


def slot_table(slots, count):
    table = lax.broadcasted_iota(jnp.int32, (count, slots.shape[1]), 0) == slots
    return table.astype(jnp.float32).astype(jnp.bfloat16)


def pack_kernel(experts, replicas, capacity, ids_ref, rows_ref, grad_ref, out_ref):
    table = slot_table(slots_of(ids_ref[...], experts, capacity), experts * capacity)
    width = rows_ref.shape[1]
    for at, ref in ((0, rows_ref), (width, grad_ref)):
        packed = jnp.dot(table, ref[...], preferred_element_type=jnp.float32).astype(jnp.bfloat16)
        packed = packed.reshape(experts, capacity, width)
        for replica in range(replicas):
            out_ref[:, replica, :, at : at + width] = packed


def pack(ids, rows, grad, experts, replicas, capacity):
    return pl.pallas_call(
        functools.partial(pack_kernel, experts, replicas, capacity),
        out_shape=jax.ShapeDtypeStruct((experts, replicas, capacity, 2 * rows.shape[1]), jnp.bfloat16),
        in_specs=[pl.BlockSpec(memory_space=VMEM)] * 3,
        out_specs=pl.BlockSpec(memory_space=VMEM),
        name="pack",
    )(ids, rows, grad)


def unpack_kernel(experts, replicas, capacity, ids_ref, parts_ref, out_ref):
    table = slot_table(slots_of(ids_ref[...], experts, capacity), experts * capacity)
    total = parts_ref[:, 0].astype(jnp.float32)
    for replica in range(1, replicas):
        total = total + parts_ref[:, replica].astype(jnp.float32)
    total = total.astype(jnp.bfloat16).reshape(experts * capacity, out_ref.shape[1])
    out_ref[...] = lax.dot_general(
        table, total, (((0,), (0,)), ((), ())), preferred_element_type=jnp.float32
    ).astype(jnp.bfloat16)


def unpack(ids, parts, experts, replicas, capacity):
    return pl.pallas_call(
        functools.partial(unpack_kernel, experts, replicas, capacity),
        out_shape=jax.ShapeDtypeStruct((ids.shape[1], parts.shape[-1]), jnp.bfloat16),
        in_specs=[pl.BlockSpec(memory_space=VMEM)] * 2,
        out_specs=pl.BlockSpec(memory_space=VMEM),
        name="unpack",
    )(ids, parts)


def expert_backward(rows_in, rows_grad, weight_first, weight_second):
    preact = jnp.dot(rows_in, weight_first, preferred_element_type=jnp.float32)
    gate_sig = jax.nn.sigmoid(preact)
    activation = (preact * gate_sig).astype(jnp.bfloat16)
    grad_act = lax.dot_general(
        rows_grad, weight_second, (((1,), (1,)), ((), ())), preferred_element_type=jnp.float32
    )
    grad_pre = (grad_act * gate_sig * (1.0 + preact * (1.0 - gate_sig))).astype(jnp.bfloat16)
    partial_value = lax.dot_general(
        grad_pre, weight_first, (((1,), (1,)), ((), ())), preferred_element_type=jnp.float32
    ).astype(jnp.bfloat16)
    grad_first = lax.dot_general(
        rows_in, grad_pre, (((0,), (0,)), ((), ())), preferred_element_type=jnp.float32
    )
    grad_second = lax.dot_general(
        activation, rows_grad, (((0,), (0,)), ((), ())), preferred_element_type=jnp.float32
    )
    return (grad_first, grad_second, partial_value)


def body(atom_rows, grad_out, expert_ids, weight_in, weight_out):
    experts = lax.axis_size("expert")
    replicas = lax.axis_size("replica")
    local_rows = atom_rows.shape[0]
    width = atom_rows.shape[1]
    capacity = 2 * local_rows // experts
    ids = expert_ids.reshape(1, local_rows)
    copies = pack(ids, atom_rows, grad_out, experts, replicas, capacity)
    copies = copies.reshape(experts * replicas, capacity, 2 * width)
    arrived = lax.all_to_all(copies, ("expert", "replica"), split_axis=0, concat_axis=0, tiled=True)
    arrived = arrived.reshape(experts * replicas * capacity, 2 * width)
    grad_first, grad_second, partial_value = expert_backward(
        arrived[:, :width], arrived[:, width:], weight_in[0], weight_out[0]
    )
    returned = lax.all_to_all(
        partial_value.reshape(experts * replicas, capacity, width),
        ("expert", "replica"),
        split_axis=0,
        concat_axis=0,
        tiled=True,
    )
    grad_rows = unpack(ids, returned.reshape(experts, replicas, capacity, width), experts, replicas, capacity)
    return (grad_rows, grad_first[None], grad_second[None])


def solution(mesh):
    return jax.shard_map(
        body,
        mesh=mesh,
        in_specs=(
            P(("expert", "replica"), None),
            P(("expert", "replica"), None),
            P(("expert", "replica"), None),
            P("expert", None, "replica"),
            P("expert", "replica", None),
        ),
        out_specs=(
            P(("expert", "replica"), None),
            P("expert", None, "replica"),
            P("expert", "replica", None),
        ),
        check_vma=False,
    )
```

time: 90.5 us -> 79 us (0.87)
  waiting for transfers between devices: 21 us -> 12.1 us
  Pallas kernels: 0 us -> 5.14 us
  matrix products: 17.8 us -> 12.7 us
  other arithmetic: 2.71 us -> 0 us
  local copies, waits for them, and re-layouts: 2.31 us -> 1.34 us
    all_to_all x1, waiting for transfers between devices: 21 us -> 12.1 us  [body(): lax.all_to_all(partial_value.reshape(experts * replicas, capacity, width)...]
    pallas_call x0 -> x2, Pallas kernels: none -> 5.14 us  [the longest x1 2.84 us: pack(): pl.pallas_call(functools.partial(pack_kernel, experts, replicas, capacity...]
    dot_general x2 -> x0, matrix products: 2.27 us -> none  [the longest x1 1.24 us: body(): jnp.dot(slot_table.astype(jnp.bfloat16), joined, preferred_element_type=j...]
    dot_general x1, matrix products: 4.85 us -> 2.66 us  [expert_backward(): lax.dot_general(activation, rows_grad, (((0,), (0,)), ((), ())), preferre...]
    reduce_sum x2 -> x0, other arithmetic: 1.05 us -> none  [the longest x1 0.83 us: pack_table(): position = jnp.sum((jnp.cumsum(onehot, axis=0) - onehot) * onehot, axis=1)]
    unnamed x12 -> x10, local copies, waits for them, and re-layouts: 2.05 us -> 1.34 us
  transfers between devices with their start and end apart: 1 -> 1, of which waited for: 1 -> 1; matrix products, arithmetic and copies ran while one was open for 11% -> 9% of each run, Pallas kernels for 0% -> 0%
where the time goes in v1:
time: 79 us; the launch traced here: 78.7 us
  blocking collectives  42 us (53%)
  matrix products  12.7 us (16%)
  waiting for transfers between devices  12.1 us (15%)
  Pallas kernels  5.14 us (7%)
  starting transfers between devices  4.71 us (6%)
  local copies, waits for them, and re-layouts  1.34 us (2%)
    all_to_all x1, blocking collectives, body(): lax.all_to_all(copies, ('expert', 'replica'), split_axis=0, concat_axis=0...  42 us
    all_to_all x1, waiting for transfers between devices, body(): lax.all_to_all(partial_value.reshape(experts * replicas, capacity, width)...  12.1 us
    all_to_all x1, starting transfers between devices, body(): lax.all_to_all(partial_value.reshape(experts * replicas, capacity, width)...  4.71 us
    dot_general x1, matrix products, expert_backward(): lax.dot_general(rows_in, grad_pre, (((0,), (0,)), ((), ())), preferred_el...  4.34 us
    pallas_call x1, Pallas kernels, pack(): pl.pallas_call(functools.partial(pack_kernel, experts, replicas, capacity...  2.84 us
    dot_general x1, matrix products, expert_backward(): lax.dot_general(activation, rows_grad, (((0,), (0,)), ((), ())), preferre...  2.66 us
    dot_general x1, matrix products, expert_backward(): lax.dot_general(grad_pre, weight_first, (((1,), (1,)), ((), ())), preferr...  2.3 us
    pallas_call x1, Pallas kernels, unpack(): pl.pallas_call(functools.partial(unpack_kernel, experts, replicas, capaci...  2.3 us
  transfers between devices with their start and end apart: 1, of which 1 were waited for; matrix products, arithmetic and copies ran while one was open for 9% of the time, Pallas kernels for 0%

profile of v1, /device:TPU:1, one launch (start us, length us, event | category | flops | bytes accessed | tf_op | source)
XLA Modules:
  0.0 78.7 jit_solution(12107216616294347854)
XLA Ops:
  0.6 0.0 copy-start
  0.6 2.8 %pack.1 = bf16[32,4,8,1024]{3,2,1,0:T(8,128)(2,1)} custom-call(s32[1,128]{1,0:T(1,128)} %bitcast.25, bf16[128,512]{1,0:T(8,128)(2,1)} %rows_ref.1, bf16[128,512]{1,0:T(8,128)(2,1)} %grad_ref.1), custom_call_target="tpu_custom_call" | custom-call | tf_op jit(solution)/shard_map/pack/pallas_call | solution.py:42
  3.5 42.0 %all_to_all.10 = bf16[128,8,1024]{2,1,0:T(8,128)(2,1)S(1)} all-to-all(bf16[128,8,1024]{2,1,0:T(8,128)(2,1)} %bitcast.20), channel_id=1, replica_groups=mesh['expert'=32,'replica'=4] {'expert','replica'}, dimensions={0} | all-to-all | bytes 4194304 | tf_op jit(solution)/shard_map/all_to_all | solution.py:101
  45.5 0.0 copy-done
  45.5 0.0 copy-start.2
  45.5 1.2 %fusion.4 = f32[1024,1024]{1,0:T(8,128)S(1)} fusion(bf16[1,512,1024]{2,1,0:T(8,128)(2,1)S(1)} %copy-done, bf16[1024,1024]{1,0:T(8,128)(2,1)S(1)} %bitcast.21), kind=kOutput, calls=%fused_computation.9 | convolution fusion | flops 1073741824 | bytes 6291456 | tf_op jit(solution)/shard_map/dot_general | solution.py:73
  46.8 0.0 copy-done.2
  46.8 0.0 copy-start.3
  46.8 2.2 %multiply_convert_fusion.1 = bf16[1024,1024]{1,0:T(8,128)(2,1)S(1)} fusion(f32[1024,1024]{1,0:T(8,128)S(1)} %fusion.4, bf16[1,1024,512]{2,1,0:T(8,128)(2,1)S(1)} %copy-done.2, bf16[1024,1024]{1,0:T(8,128)(2,1)S(1)} %bitcast.22), kind=kOutput, calls=%fused_computation.1 | convolution fusion | flops 1083179008 | bytes 8388608 | tf_op jit(solution)/shard_map/dot_general | solution.py:76
  49.0 0.0 copy-done.3
  49.0 0.0 copy-start.1
  49.0 1.3 %copy-done.1 = bf16[1024,1024]{1,0:T(8,128)(2,1)} copy-done((bf16[1024,1024]{1,0:T(8,128)(2,1)}, bf16[1024,1024]{1,0:T(8,128)(2,1)S(1)}, u32[]{:S(2)}) %copy-start.1) | copy-done | bytes 2097176
  50.3 2.3 %fusion.2 = bf16[128,8,512]{2,1,0:T(8,128)(2,1)} fusion(bf16[1024,1024]{1,0:T(8,128)(2,1)S(1)} %multiply_convert_fusion.1, bf16[1,512,1024]{2,1,0:T(8,128)(2,1)S(1)} %copy-done), kind=kOutput, calls=%fused_computation.7 | convolution fusion | flops 1074266112 | bytes 4194304 | tf_op jit(solution)/shard_map/dot_general | solution.py:80
  52.6 4.7 %all-to-all-start.1 = ((bf16[128,8,512]{2,1,0:T(8,128)(2,1)}), bf16[128,8,512]{2,1,0:T(8,128)(2,1)}, u32[]{:S(2)}, u32[]{:S(2)}) async-start(bf16[128,8,512]{2,1,0:T(8,128)(2,1)} %fusion.2), calls=%async_computation.1 | async-start | bytes 2097152 | tf_op jit(solution)/shard_map/all_to_all | solution.py:106
  57.3 0.0 copy-start.4
  57.3 4.3 %convolution_bitcast_fusion = f32[1,512,1024]{2,1,0:T(8,128)} fusion(bf16[1024,1024]{1,0:T(8,128)(2,1)} %copy-done.1, bf16[1024,1024]{1,0:T(8,128)(2,1)S(1)} %bitcast.23), kind=kOutput, calls=%fused_computation.4 | convolution fusion | flops 1073741824 | bytes 5242880 | tf_op jit(solution)/shard_map/dot_general | solution.py:83
  61.7 0.0 copy-done.4
  61.7 2.7 %fusion.1 = f32[1,1024,512]{2,1,0:T(8,128)} fusion(f32[1024,1024]{1,0:T(8,128)S(1)} %copy-done.4, bf16[1024,1024]{1,0:T(8,128)(2,1)S(1)} %bitcast.24), kind=kOutput, calls=%fused_computation.5 | convolution fusion | flops 1078984704 | bytes 7340032 | tf_op jit(solution)/shard_map/dot_general | solution.py:86
  64.3 12.1 %all-to-all-done.1 = bf16[128,8,512]{2,1,0:T(8,128)(2,1)} async-done(((bf16[128,8,512]{2,1,0:T(8,128)(2,1)}), bf16[128,8,512]{2,1,0:T(8,128)(2,1)}, u32[]{:S(2)}, u32[]{:S(2)}) %all-to-all-start.1) | async-done | bytes 1048608 | tf_op jit(solution)/shard_map/all_to_all | solution.py:106
  76.4 2.3 %unpack.1 = bf16[128,512]{1,0:T(8,128)(2,1)} custom-call(s32[1,128]{1,0:T(1,128)} %bitcast.26, bf16[32,4,8,512]{3,2,1,0:T(8,128)(2,1)} %bitcast.6.parts_ref), custom_call_target="tpu_custom_call" | custom-call | tf_op jit(solution)/shard_map/unpack/pallas_call | solution.py:63
Async XLA Ops:
  0.6 44.9 %copy-start = (bf16[1,512,1024]{2,1,0:T(8,128)(2,1)S(1)}, bf16[1,512,1024]{2,1,0:T(8,128)(2,1)}, u32[]{:S(2)}) copy-start(bf16[1,512,1024]{2,1,0:T(8,128)(2,1)} %param.8) | copy-start | bytes 3145732
  45.5 1.3 %copy-start.2 = (bf16[1,1024,512]{2,1,0:T(8,128)(2,1)S(1)}, bf16[1,1024,512]{2,1,0:T(8,128)(2,1)}, u32[]{:S(2)}) copy-start(bf16[1,1024,512]{2,1,0:T(8,128)(2,1)} %param.9) | copy-start | bytes 3145732
  46.8 2.2 %copy-start.3 = (f32[1024,1024]{1,0:T(8,128)}, f32[1024,1024]{1,0:T(8,128)S(1)}, u32[]{:S(2)}) copy-start(f32[1024,1024]{1,0:T(8,128)S(1)} %fusion.4) | copy-start | bytes 12582916
  49.0 1.3 %copy-start.1 = (bf16[1024,1024]{1,0:T(8,128)(2,1)}, bf16[1024,1024]{1,0:T(8,128)(2,1)S(1)}, u32[]{:S(2)}) copy-start(bf16[1024,1024]{1,0:T(8,128)(2,1)S(1)} %multiply_convert_fusion.1) | copy-start | bytes 6291460
  52.6 23.8 %all-to-all-start.1 = ((bf16[128,8,512]{2,1,0:T(8,128)(2,1)}), bf16[128,8,512]{2,1,0:T(8,128)(2,1)}, u32[]{:S(2)}, u32[]{:S(2)}) async-start(bf16[128,8,512]{2,1,0:T(8,128)(2,1)} %fusion.2), calls=%async_computation.1 | async-start | bytes 2097152 | tf_op jit(solution)/shard_map/all_to_all | solution.py:106
  57.3 4.4 %copy-start.4 = (f32[1024,1024]{1,0:T(8,128)S(1)}, f32[1024,1024]{1,0:T(8,128)}, u32[]{:S(2)}) copy-start(f32[1024,1024]{1,0:T(8,128)} %copy-done.3) | copy-start | bytes 12582916
